TPU v7x, 256 devices: a whole 4x4x8 slice. The times are simulated.
256 devices in a mesh: tok: 16 (over z, y_hi), feat: 4 (over x), pb: 4 (over y_lo, core).
Axes of the slice: x: 4, y: 4 (y_hi: 2, y_lo: 2; y = y_hi * 2 + y_lo), z: 8, core: 2. Of those that a mesh axis runs over, the one named last changes fastest.
Arguments:
- out_grads: bfloat16 [81920, 8192], P(('tok', 'pb'), 'feat'), may hold values from -6 to 6
- acts: bfloat16 [81920, 8192], P(('tok', 'pb'), 'feat'), may hold values from -6 to 6
- s_inverse: bfloat16 [8192, 8192], P('feat', ('tok', 'pb')), may hold values from -1 to 3, as said below
- a_inverse: bfloat16 [8192, 8192], P('feat', ('tok', 'pb')), may hold values from -1 to 3, as said below
- query_out: bfloat16 [8192, 512], P(('tok', 'pb')), may hold values from -0.0625 to 0.0625
- query_in: bfloat16 [8192, 512], P(('tok', 'pb')), may hold values from -0.0625 to 0.0625
Outputs:
- scores: float32 [32, 81920], P('feat', ('tok', 'pb'))
Inputs may be any that keep to these rules, and one draw needn't show every extreme that they name: `s_inverse`: symmetric; diagonal entries roughly between 0.5 and 2. `a_inverse`: symmetric; diagonal entries roughly between 0.5 and 2.
All inputs are finite; a program needn't handle non-finite values.
Results may differ from a plain program's by a relative error of at most 0.0041.
Values may be sent and summed in bfloat16 or wider, within the bound.
A program may use at most 128 MiB of HBM per device.

v0:
```python
import jax
import jax.numpy as jnp
from jax import lax
from jax.sharding import PartitionSpec as P

RANK = 16


def side_by_side(arrays, axis, dim, along):
    both = jnp.concatenate(arrays, axis=along)
    result, at, outs = (lax.all_gather(both, axis, axis=dim, tiled=True), 0, [])
    for a in arrays:
        outs.append(lax.slice_in_dim(result, at, at + a.shape[along], axis=along))
        at += a.shape[along]
    return tuple(outs)


def in_one_piece(arrays, axis, dim, along):
    both = jnp.concatenate(arrays, axis=along)
    result, at, outs = (lax.psum_scatter(both, axis, scatter_dimension=dim, tiled=True), 0, [])
    for a in arrays:
        outs.append(lax.slice_in_dim(result, at, at + a.shape[along], axis=along))
        at += a.shape[along]
    return tuple(outs)


def per_device(out_grads, acts, s_inverse, a_inverse, query_out, query_in):
    s_rows, a_rows = (
        lax.all_to_all(s_inverse, ("tok", "pb"), split_axis=0, concat_axis=1, tiled=True),
        lax.all_to_all(a_inverse, ("tok", "pb"), split_axis=0, concat_axis=1, tiled=True),
    )
    out_full, in_full = side_by_side((query_out, query_in), ("tok", "pb"), 0, 1)
    left_rows = jnp.dot(s_rows, out_full, preferred_element_type=jnp.float32)
    right_rows = jnp.dot(a_rows, in_full, preferred_element_type=jnp.float32)
    left_rows = left_rows.astype(jnp.bfloat16)
    right_rows = right_rows.astype(jnp.bfloat16)
    token_rows = out_grads.shape[0]
    width = left_rows.shape[1]
    left_block, right_block = side_by_side((left_rows, right_rows), ("tok", "pb"), 0, 1)
    grad_part = jnp.dot(out_grads, left_block, preferred_element_type=jnp.float32)
    act_part = jnp.dot(acts, right_block, preferred_element_type=jnp.float32)
    feat_count = lax.axis_size("feat")
    share = width // feat_count
    grad_proj, act_proj = in_one_piece((grad_part, act_part), "feat", 1, 0)
    scale = 1.0 / RANK**0.5
    summed = (grad_proj * act_proj).reshape(token_rows, share // RANK, RANK).sum(axis=2)
    return (summed * scale).T


def solution(mesh):
    placed = (
        P(("tok", "pb"), "feat"),
        P(("tok", "pb"), "feat"),
        P("feat", ("tok", "pb")),
        P("feat", ("tok", "pb")),
        P(("tok", "pb"), None),
        P(("tok", "pb"), None),
    )
    return jax.shard_map(
        per_device, mesh=mesh, in_specs=placed, out_specs=P("feat", ("tok", "pb")), check_vma=False
    )
```

profile of v0, /device:TPU:3, one launch (start us, length us, event | category | flops | bytes accessed | tf_op | source)
XLA Modules:
  0.0 282.8 jit_solution(7685651976250139549)
XLA Ops:
  6.5 0.0 all-gather.3.cloned.1.call-start
  6.5 1.7 pad_maximum_fusion.1
  8.2 0.0 all-gather.3.cloned.1.call-update
  8.3 32.6 %all_to_all.38 = bf16[64,32,128]{2,1,0:T(8,128)(2,1)S(1)} all-to-all(bf16[64,32,128]{2,1,0:T(8,128)(2,1)} %bitcast.32), channel_id=1, replica_groups=mesh['tok'=16,'feat'=4,'pb'=4] {'tok','pb'}, dimensions={0} | all-to-all | bytes 1048576 | tf_op jit(solution)/shard_map/all_to_all | solution.py:30
  40.8 5.5 %all-to-all-start = ((bf16[64,32,128]{2,1,0:T(8,128)(2,1)}), bf16[64,32,128]{2,1,0:T(8,128)(2,1)S(1)}, u32[]{:S(2)}, u32[]{:S(2)}) async-start(bf16[64,32,128]{2,1,0:T(8,128)(2,1)} %bitcast.33), calls=%async_computation | async-start | bytes 1048576 | tf_op jit(solution)/shard_map/all_to_all | solution.py:29
  46.3 0.0 all-gather.5.cloned.1.call-start
  46.4 72.7 %all-gather.3.cloned.1.call-done = bf16[8192,1024]{1,0:T(8,128)(2,1)} async-done(((bf16[128,1024]{1,0:T(8,128)(2,1)}), bf16[8192,1024]{1,0:T(8,128)(2,1)}) %all-gather.3.cloned.1.call-update) | async-done | bytes 16777232 | tf_op jit(solution)/shard_map/all_gather | solution.py:11
  119.1 4.9 %fusion.12 = bf16[32,512]{1,0:T(8,128)(2,1)S(1)} fusion(bf16[8192,1024]{1,0:T(8,128)(2,1)} %all-gather.3.cloned.1.call-done, bf16[64,32,128]{2,1,0:T(8,128)(2,1)S(1)} %all_to_all.38), kind=kOutput, calls=%fused_computation.11 | convolution fusion | flops 268451840 | bytes 8945664 | tf_op jit(solution)/shard_map/dot_general | solution.py:34
  124.0 0.0 all-to-all-done
  124.0 4.9 %fusion.15 = bf16[32,512]{1,0:T(8,128)(2,1)S(1)} fusion(bf16[8192,1024]{1,0:T(8,128)(2,1)} %all-gather.3.cloned.1.call-done, bf16[64,32,128]{2,1,0:T(8,128)(2,1)S(1)} %all-to-all-done), kind=kOutput, calls=%fused_computation.12 | convolution fusion | flops 268451840 | bytes 8945664 | tf_op jit(solution)/shard_map/dot_general | solution.py:33
  128.9 0.7 pad_maximum_fusion.2
  129.6 0.0 all-gather.5.cloned.1.call-update
  129.6 0.0 reduce-scatter.2.cloned.1.call-start
  129.7 76.1 %all-gather.5.cloned.1.call-done = bf16[2048,1024]{1,0:T(8,128)(2,1)} async-done(((bf16[32,1024]{1,0:T(8,128)(2,1)}), bf16[2048,1024]{1,0:T(8,128)(2,1)}) %all-gather.5.cloned.1.call-update) | async-done | bytes 4194320 | tf_op jit(solution)/shard_map/all_gather | solution.py:11
  205.8 0.0 copy-start
  205.8 6.2 %convolution_bitcast_fusion = f32[1280,512]{0,1:T(8,128)S(1)} fusion(bf16[1280,2048]{1,0:T(8,128)(2,1)} %param.7, bf16[2048,1024]{1,0:T(8,128)(2,1)} %all-gather.5.cloned.1.call-done), kind=kOutput, calls=%fused_computation.5 | convolution fusion | flops 2684354560 | bytes 9961472 | tf_op jit(solution)/shard_map/dot_general | solution.py:41
  212.0 0.0 copy-done
  212.0 5.5 %convolution_bitcast_fusion.1 = f32[1280,512]{0,1:T(8,128)S(1)} fusion(bf16[1280,2048]{1,0:T(8,128)(2,1)} %param.6, bf16[2048,1024]{1,0:T(8,128)(2,1)S(1)} %copy-done), kind=kOutput, calls=%fused_computation.6 | convolution fusion | flops 2684354560 | bytes 9961472 | tf_op jit(solution)/shard_map/dot_general | solution.py:40
  217.5 2.9 %pad_maximum_fusion = f32[2560,512]{0,1:T(8,128)} fusion(f32[1280,512]{0,1:T(8,128)S(1)} %convolution_bitcast_fusion, f32[1280,512]{0,1:T(8,128)S(1)} %convolution_bitcast_fusion.1), kind=kLoop, calls=%fused_computation.4 | loop fusion | flops 1310720 | bytes 10485760 | tf_op jit(solution)/shard_map/concatenate | solution.py:19
  220.5 0.0 reduce-scatter.2.cloned.1.call-update
  220.5 53.7 %reduce-scatter.2.cloned.1.call-done = f32[2560,128]{0,1:T(8,128)} async-done(((f32[2560,512]{0,1:T(8,128)}), f32[2560,128]{0,1:T(8,128)}) %reduce-scatter.2.cloned.1.call-update) | async-done | bytes 1310736 | tf_op jit(solution)/shard_map/reduce_scatter | solution.py:20
  274.2 1.4 bitcast_reduce_fusion
  275.6 0.6 multiply_bitcast_fusion
Async XLA Ops:
  6.5 112.6 %all-gather.3.cloned.1.call-start = ((), (), s32[]{:S(2)}) async-start(), calls=%async_computation.3 | async-start | bytes 17039360 | tf_op jit(solution)/shard_map/all_gather | solution.py:11
  40.8 83.2 %all-to-all-start = ((bf16[64,32,128]{2,1,0:T(8,128)(2,1)}), bf16[64,32,128]{2,1,0:T(8,128)(2,1)S(1)}, u32[]{:S(2)}, u32[]{:S(2)}) async-start(bf16[64,32,128]{2,1,0:T(8,128)(2,1)} %bitcast.33), calls=%async_computation | async-start | bytes 1048576 | tf_op jit(solution)/shard_map/all_to_all | solution.py:29
  46.3 159.5 %all-gather.5.cloned.1.call-start = ((), (), s32[]{:S(2)}) async-start(), calls=%async_computation.4 | async-start | bytes 4259840 | tf_op jit(solution)/shard_map/all_gather | solution.py:11
  129.6 144.6 %reduce-scatter.2.cloned.1.call-start = ((), (), s32[]{:S(2)}) async-start(), calls=%async_computation.5 | async-start | bytes 6553600 | tf_op jit(solution)/shard_map/reduce_scatter | solution.py:20
  205.8 6.2 %copy-start = (bf16[2048,1024]{1,0:T(8,128)(2,1)S(1)}, bf16[2048,1024]{1,0:T(8,128)(2,1)}, u32[]{:S(2)}) copy-start(bf16[2048,1024]{1,0:T(8,128)(2,1)} %all-gather.5.cloned.1.call-done) | copy-start | bytes 12582916
Sparse Core Ops, SparseCore 0:
  10.1 108.9 all-gather.2
  129.7 76.0 all-gather.4
  220.6 53.5 reduce-scatter.1
where the time goes:
time: 285 us; the launch traced here: 283 us
  waiting for transfers between devices  203 us (71%)
  blocking collectives  32.6 us (11%)
  matrix products  21.5 us (8%)
  between operations  13.1 us (5%)
  other arithmetic  7.33 us (3%)
  starting transfers between devices  5.56 us (2%)
    all_gather x2, waiting for transfers between devices, side_by_side(): result, at, outs = (lax.all_gather(both, axis, axis=dim, tiled=True), 0, [])  149 us
    reduce_scatter x1, waiting for transfers between devices, in_one_piece(): lax.psum_scatter(both, axis, scatter_dimension=dim, tiled=True)  53.7 us
    all_to_all x1, blocking collectives, per_device(): lax.all_to_all(a_inverse, ('tok', 'pb'), split_axis=0, concat_axis=1, til...  32.6 us
    dot_general x1, matrix products, per_device(): act_part = jnp.dot(acts, right_block, preferred_element_type=jnp.float32)  6.18 us
  transfers between devices with their start and end apart: 4, of which 3 were waited for; matrix products, arithmetic and copies ran while one was open for 2% of the time, Pallas kernels for 0%

commit v1 on v0

v1 whole, which is shorter than its diff:
```python
import functools

import jax
import jax.numpy as jnp
from jax import lax
from jax.experimental import pallas as pl
from jax.experimental.pallas import tpu as pltpu
from jax.sharding import PartitionSpec as P

RANK = 16
MESH = pl.DeviceIdType.MESH
BF16, F32 = jnp.bfloat16, jnp.float32
ROWS = 1280
HALF = ROWS // 2
TILE = 320


def place(x, y, z, k):
    return (z * 2 + lax.div(y, 2), x, lax.rem(y, 2) * 2 + k)


def kernel(
    grads, acts, s_inv, a_inv, q_out, q_in, out,
    xv, mbuf, mt, qv, qrel, qg, part, cbuf, lq, both, own, opp, near, hrecv, frecv,
    l_sem, m_send, m_recv, a_send, a_recv, b_send, b_recv, c_send, c_recv,
    d_send, d_recv, e_send, e_recv, f_send, f_recv, h_send, h_recv, n_send, n_recv,
):
    tok, x, pb = lax.axis_index("tok"), lax.axis_index("feat"), lax.axis_index("pb")
    z, k = lax.div(tok, 2), lax.rem(pb, 2)
    y = lax.rem(tok, 2) * 2 + lax.div(pb, 2)
    home, z2 = lax.div(z, 2), lax.rem(z, 2)
    at_home = home == x

    def xs(d):
        return lax.rem(x + d, 4)

    def ys(d):
        return lax.rem(y + d, 4)

    x_dev = [None] + [place(xs(d), y, z, k) for d in (1, 2, 3)]
    y_dev = [None] + [place(x, ys(d), z, k) for d in (1, 2, 3)]
    twin = place(x, y, z, 1 - k)

    def local(src, dst, sem):
        return pltpu.make_async_copy(src, dst, sem)

    def remote(src, dst, send, recv, dev):
        return pltpu.make_async_remote_copy(
            src_ref=src, dst_ref=dst, send_sem=send, recv_sem=recv,
            device_id=dev, device_id_type=MESH,
        )

    q_rows = pl.ds(pl.multiple_of(x * 32, 32), 32)
    load_q = [local(q.at[q_rows, :], qv.at[m], l_sem.at[m]) for m, q in enumerate((q_out, q_in))]
    for c in load_q:
        c.start()

    @pl.when(k == 0)
    def _():
        local(s_inv, mbuf.at[0], l_sem.at[2]).start()

    @pl.when(k == 1)
    def _():
        local(a_inv, mbuf.at[1], l_sem.at[2]).start()

    load_x = [local(t, xv.at[m], l_sem.at[3 + m]) for m, t in enumerate((grads, acts))]
    for c in load_x:
        c.start()

    barrier = pltpu.get_barrier_semaphore()

    def greet(dev):
        pl.semaphore_signal(barrier, inc=1, device_id=dev, device_id_type=MESH)

    def greet_source(i, carry):
        sx, sz, sk = lax.div(i, 4), 2 * x + lax.rem(lax.div(i, 2), 2), lax.rem(i, 2)
        me = (sx == x) & (sz == z) & (sk == k)

        @pl.when(jnp.logical_not(me))
        def _():
            greet(place(sx, y, sz, sk))

        return carry

    lax.fori_loop(0, 16, greet_source, 0)
    for dev in (y_dev[1], y_dev[3], x_dev[1], x_dev[2], x_dev[3], twin):
        greet(dev)
    pl.semaphore_wait(barrier, 22 - at_home.astype(jnp.int32))

    @pl.when(k == 0)
    def _():
        remote(a_inv, mbuf.at[0], m_send, m_recv, twin).start()

    @pl.when(k == 1)
    def _():
        remote(s_inv, mbuf.at[1], m_send, m_recv, twin).start()

    for c in load_q:
        c.wait()
    for m in range(2):
        for plane in range(4):
            for j, d in enumerate((2, 0, 1, 3)):
                col = (plane + d) % 4 * 128
                qrel[m, plane, :, 128 * j:128 * j + 128] = qv[m, :, col:col + 128]

    q_dst_rows = pl.ds(pl.multiple_of(k * 128 + x * 32, 32), 32)

    def a_copy(h, i):
        zt, kt = lax.rem(z + 4 + lax.div(i, 2), 8), lax.rem(i, 2)
        me = at_home & (zt == z) & (kt == k)
        src = qrel.at[kt, lax.div(zt, 2), :, pl.ds(256 * h, 256)]
        dst = qg.at[h, z2, y, q_dst_rows, :]
        far = remote(src, dst, a_send.at[h, i], a_recv.at[h], place(home, y, zt, kt))
        return me, local(src, dst, a_recv.at[h]), far

    for h in range(2):
        def a_start(i, carry, h=h):
            me, near_copy, far = a_copy(h, i)

            @pl.when(me)
            def _():
                near_copy.start()

            @pl.when(jnp.logical_not(me))
            def _():
                far.start()

            return carry

        lax.fori_loop(0, 16, a_start, 0)

    local(mbuf.at[k], mbuf.at[k], l_sem.at[2]).wait()
    mt[pl.ds(pl.multiple_of(k * 128, 128), 128), :] = mbuf[k].T
    remote(mbuf.at[1 - k], mbuf.at[1 - k], m_send, m_recv, twin).wait_recv()
    mt[pl.ds(pl.multiple_of((1 - k) * 128, 128), 128), :] = mbuf[1 - k].T

    def spread(buf, h, send, recv):
        mine = buf.at[h, :, y]
        up = remote(mine, mine, send.at[h, 0], recv.at[h, 0], y_dev[1])
        down = remote(mine, mine, send.at[h, 1], recv.at[h, 1], y_dev[3])
        up.start()
        down.start()
        return [up, down]

    def landed(buf, h, recv, side):
        block = buf.at[h, :, ys(3) if side == 0 else ys(1)]
        remote(block, block, recv.at[h, side], recv.at[h, side], y_dev[1]).wait_recv()

    def pass_on(buf, h, send, recv, side):
        half = buf.at[h, side, ys(3) if side == 0 else ys(1)]
        c = remote(half, half, send.at[h, 2 + side], recv.at[h, 2 + side],
                   y_dev[1] if side == 0 else y_dev[3])
        c.start()
        return c

    def landed_far(buf, h, recv, side):
        half = buf.at[h, side, ys(2)]
        remote(half, half, recv.at[h, 2 + side], recv.at[h, 2 + side], y_dev[1]).wait_recv()

    sent = []
    for h in range(2):
        block = qg.at[h, :, y]
        local(block, block, a_recv.at[h]).wait()
        sent += spread(qg, h, b_send, b_recv)

    for h in range(2):
        for side in range(2):
            landed(qg, h, b_recv, side)
            sent.append(pass_on(qg, h, b_send, b_recv, side))
        for side in range(2):
            landed_far(qg, h, b_recv, side)
        part[h] = jnp.dot(mt[...], qg[h].reshape(2048, 256), preferred_element_type=F32)
        for d in (1, 2, 3):
            rows = pl.ds(pl.multiple_of(xs(d) * 64, 64), 64)
            c = remote(part.at[h, rows, :], cbuf.at[h, d - 1], c_send.at[h, d - 1],
                       c_recv.at[h, d - 1], x_dev[d])
            c.start()
            sent.append(c)

    mine64 = pl.ds(pl.multiple_of(x * 64, 64), 64)
    mb = both.at[k]

    def d_copy(h, i):
        zt = lax.rem(z + 4 + i, 8)
        me = at_home & (zt == z)
        dst = mb.at[h, z2, y, mine64, :]
        far = remote(lq.at[h], dst, d_send.at[h, i], d_recv.at[h], place(home, y, zt, k))
        return me, local(lq.at[h], dst, d_recv.at[h]), far

    for h in range(2):
        for d in range(3):
            c = cbuf.at[h, d]
            remote(c, c, c_recv.at[h, d], c_recv.at[h, d], x_dev[1]).wait_recv()
        total = part[h, mine64, :] + cbuf[h, 0] + cbuf[h, 1] + cbuf[h, 2]
        lq[h] = total.astype(BF16)

        def d_start(i, carry, h=h):
            me, near_copy, far = d_copy(h, i)

            @pl.when(me)
            def _():
                near_copy.start()

            @pl.when(jnp.logical_not(me))
            def _():
                far.start()

            return carry

        lax.fori_loop(0, 8, d_start, 0)

    def to_twin(h, b):
        block = mb.at[h, :, ys(b)]
        c = remote(block, block, f_send.at[h, b], f_recv.at[h, b], twin)
        c.start()
        sent.append(c)

    for h in range(2):
        block = mb.at[h, :, y]
        local(block, block, d_recv.at[h]).wait()
        sent.extend(spread(mb, h, e_send, e_recv))
        to_twin(h, 0)

    def gather_block(h):
        for side in range(2):
            landed(mb, h, e_recv, side)
            sent.append(pass_on(mb, h, e_send, e_recv, side))
            to_twin(h, 3 if side == 0 else 1)
        for side in range(2):
            landed_far(mb, h, e_recv, side)
        to_twin(h, 2)

    def twin_block(h):
        for b in range(4):
            block = both.at[1 - k, h, :, ys(b)]
            remote(block, block, f_recv.at[h, b], f_recv.at[h, b], twin).wait_recv()

    def project(m, h, tile):
        rows = pl.ds(pl.multiple_of(tile * TILE, TILE), TILE)
        w = both[m, h].reshape(2048, 256)
        return rows, jnp.dot(xv[m, rows, :], w, preferred_element_type=F32)

    gather_block(0)
    for turn in range(2):
        m = k if turn == 0 else 1 - k
        if turn == 0:
            for c in load_x:
                c.wait()
        else:
            twin_block(0)

        def first(tile, carry, m=m):
            rows, acc = project(m, 0, tile)
            opp[m, rows, :] = acc[:, :128].astype(BF16)
            own[m, rows, :] = acc[:, 128:]
            return carry

        lax.fori_loop(0, 4, first, 0)
        for side, d in ((0, 1), (1, 3)):
            c = remote(opp.at[m, pl.ds(HALF * (1 - side), HALF), :], hrecv.at[side, m],
                       h_send.at[turn, side], h_recv.at[m, side], x_dev[d])
            c.start()
            sent.append(c)

    gather_block(1)
    for turn in range(2):
        m = k if turn == 0 else 1 - k
        if turn == 1:
            twin_block(1)
        for side in range(2):
            c = hrecv.at[side, m]
            remote(c, c, h_recv.at[m, side], h_recv.at[m, side], x_dev[1]).wait_recv()
        for part_at in range(2):
            def second(tile, carry, m=m, part_at=part_at):
                rows, acc = project(m, 1, tile + 2 * part_at)
                inner = pl.ds(pl.multiple_of(tile * TILE, TILE), TILE)
                side = 1 - part_at
                more = hrecv[side, m, inner, :].astype(F32)
                for j in range(2):
                    piece = acc[:, 128 * j:128 * j + 128]
                    if j == side:
                        piece = piece + more
                    near[j, m, rows, :] = piece.astype(BF16)
                return carry

            lax.fori_loop(0, 2, second, 0)
            rows = pl.ds(HALF * part_at, HALF)
            for j, d in ((0, 1), (1, 3)):
                c = remote(near.at[j, m, rows, :], frecv.at[j, m, rows, :],
                           n_send.at[turn, part_at, j], n_recv.at[m, part_at, j], x_dev[d])
                c.start()
                sent.append(c)

    lane = lax.broadcasted_iota(jnp.int32, (8, 128), 1)
    query = lax.broadcasted_iota(jnp.int32, (8, 128), 0)
    pick = jnp.where(lax.div(lane, RANK) == query, 1.0, 0.0).astype(F32)
    for part_at in range(2):
        rows = pl.ds(HALF * part_at, HALF)
        for m in range(2):
            for j in range(2):
                c = frecv.at[j, m, rows, :]
                remote(c, c, n_recv.at[m, part_at, j], n_recv.at[m, part_at, j], x_dev[1]).wait_recv()
        g, a = (own[m, rows, :] + frecv[0, m, rows, :].astype(F32) + frecv[1, m, rows, :].astype(F32)
                for m in range(2))
        prod = g * a * (1.0 / RANK**0.5)
        out[:, rows] = lax.dot_general(
            pick, prod, (((1,), (1,)), ((), ())),
            precision=lax.Precision.HIGHEST, preferred_element_type=F32,
        )

    for c in sent:
        c.wait_send()
    remote(mbuf.at[k], mbuf.at[k], m_send, m_recv, twin).wait_send()
    for h in range(2):
        def a_sent(i, carry, h=h):
            me, _, far = a_copy(h, i)

            @pl.when(jnp.logical_not(me))
            def _():
                far.wait_send()

            return carry

        lax.fori_loop(0, 16, a_sent, 0)

        def d_sent(i, carry, h=h):
            me, _, far = d_copy(h, i)

            @pl.when(jnp.logical_not(me))
            def _():
                far.wait_send()

            return carry

        lax.fori_loop(0, 8, d_sent, 0)


def per_device(out_grads, acts, s_inverse, a_inverse, query_out, query_in):
    dma = pltpu.SemaphoreType.DMA
    vmem = pltpu.VMEM
    return pl.pallas_call(
        kernel,
        out_shape=jax.ShapeDtypeStruct((8, ROWS), F32),
        in_specs=[pl.BlockSpec(memory_space=pl.ANY)] * 6,
        out_specs=pl.BlockSpec(memory_space=pltpu.VMEM),
        scratch_shapes=[
            vmem((2, ROWS, 2048), BF16),
            vmem((2, 2048, 128), BF16),
            vmem((256, 2048), BF16),
            vmem((2, 32, 512), BF16),
            vmem((2, 4, 32, 512), BF16),
            vmem((2, 2, 4, 256, 256), BF16),
            vmem((2, 256, 256), F32),
            vmem((2, 3, 64, 256), F32),
            vmem((2, 64, 256), BF16),
            vmem((2, 2, 2, 4, 256, 256), BF16),
            vmem((2, ROWS, 128), F32),
            vmem((2, ROWS, 128), BF16),
            vmem((2, 2, ROWS, 128), BF16),
            vmem((2, 2, HALF, 128), BF16),
            vmem((2, 2, ROWS, 128), BF16),
            dma((5,)), dma, dma, dma((2, 16)), dma((2,)), dma((2, 4)), dma((2, 4)),
            dma((2, 3)), dma((2, 3)), dma((2, 8)), dma((2,)), dma((2, 4)), dma((2, 4)),
            dma((2, 4)), dma((2, 4)), dma((2, 2)), dma((2, 2)), dma((2, 2, 2)), dma((2, 2, 2)),
        ],
        compiler_params=pltpu.CompilerParams(
            collective_id=0, has_side_effects=True, vmem_limit_bytes=52 * 1024 * 1024
        ),
    )(out_grads, acts, s_inverse, a_inverse, query_out, query_in)


def solution(mesh):
    placed = (
        P(("tok", "pb"), "feat"),
        P(("tok", "pb"), "feat"),
        P("feat", ("tok", "pb")),
        P("feat", ("tok", "pb")),
        P(("tok", "pb"), None),
        P(("tok", "pb"), None),
    )
    return jax.shard_map(
        per_device, mesh=mesh, in_specs=placed, out_specs=P("feat", ("tok", "pb")), check_vma=False
    )
```

time: 285 us -> 101 us (0.35)
  waiting for transfers between devices: 203 us -> 0 us
  Pallas kernels: 0 us -> 94.3 us
  blocking collectives: 32.6 us -> 0 us
  matrix products: 21.5 us -> 0 us
  between operations: 13.1 us -> 0.01 us
  other arithmetic: 7.33 us -> 0 us
  starting transfers between devices: 5.56 us -> 0 us
  local copies, waits for them, and re-layouts: 0.01 us -> 4.51 us
    all_gather x2 -> x0, waiting for transfers between devices: 149 us -> none  [side_by_side(): result, at, outs = (lax.all_gather(both, axis, axis=dim, tiled=True), 0, [])]
    pallas_call x0 -> x1, Pallas kernels: none -> 94.3 us  [per_device(): pl.pallas_call(kernel, out_shape=jax.ShapeDtypeStruct((8, ROWS), F32), in...]
    reduce_scatter x1 -> x0, waiting for transfers between devices: 53.7 us -> none  [in_one_piece(): lax.psum_scatter(both, axis, scatter_dimension=dim, tiled=True)]
    all_to_all x1 -> x0, blocking collectives: 32.6 us -> none  [per_device(): lax.all_to_all(a_inverse, ('tok', 'pb'), split_axis=0, concat_axis=1, til...]
    dot_general x4 -> x0, matrix products: 21.5 us -> none  [the longest x1 6.18 us: per_device(): act_part = jnp.dot(acts, right_block, preferred_element_type=jnp.float32)]
    all_to_all x1 -> x0, starting transfers between devices: 5.48 us -> none  [per_device(): lax.all_to_all(s_inverse, ('tok', 'pb'), split_axis=0, concat_axis=1, til...]
    concatenate x3 -> x0, other arithmetic: 5.29 us -> none  [the longest x1 2.94 us: in_one_piece(): both = jnp.concatenate(arrays, axis=along)]
    unnamed x2 -> x9, local copies, waits for them, and re-layouts: 0.01 us -> 4.51 us
  transfers between devices with their start and end apart: 4 -> 0, of which waited for: 3 -> 0; matrix products, arithmetic and copies ran while one was open for 2% -> 0% of each run, Pallas kernels for 0% -> 0%
where the time goes in v1:
time: 101 us; the launch traced here: 98.8 us
  Pallas kernels  94.3 us (93%)
  local copies, waits for them, and re-layouts  4.51 us (4%)
    pallas_call x1, Pallas kernels, per_device(): pl.pallas_call(kernel, out_shape=jax.ShapeDtypeStruct((8, ROWS), F32), in...  94.3 us
    unnamed x9, local copies, waits for them, and re-layouts  4.51 us

profile of v1, /device:TPU:3, one launch (start us, length us, event | category | flops | bytes accessed | tf_op | source)
XLA Modules:
  0.0 98.8 jit_solution(4114454614829953658)
XLA Ops:
  0.0 0.0 copy-start
  0.0 1.0 %copy-done = bf16[2048,128]{1,0:T(8,128)(2,1)S(1)} copy-done((bf16[2048,128]{1,0:T(8,128)(2,1)S(1)}, bf16[2048,128]{1,0:T(8,128)(2,1)}, u32[]{:S(2)}) %copy-start) | copy-done | bytes 524312
  1.0 0.0 copy-start.1
  1.0 1.0 %copy-done.1 = bf16[2048,128]{1,0:T(8,128)(2,1)S(1)} copy-done((bf16[2048,128]{1,0:T(8,128)(2,1)S(1)}, bf16[2048,128]{1,0:T(8,128)(2,1)}, u32[]{:S(2)}) %copy-start.1) | copy-done | bytes 524312
  2.1 0.0 copy-start.2
  2.1 0.9 copy-done.2
  3.0 0.0 copy-start.3
  3.0 0.9 copy-done.3
  3.9 94.3 %shard_map.64 = f32[8,1280]{1,0:T(8,128)S(1)} custom-call(bf16[1280,2048]{1,0:T(8,128)(2,1)} %grads.1, bf16[1280,2048]{1,0:T(8,128)(2,1)} %acts.1, bf16[2048,128]{1,0:T(8,128)(2,1)S(1)} %copy-done, bf16[2048,128]{1,0:T(8,128)(2,1)S(1)} %copy-done.1, bf16[128,512]{1,0:T(8,128)(2,1)S(1)} %copy-done.2, bf16[128,512]{1,0:T(8,128)(2,1)S(1)} %copy-done.3), custom_call_target="tpu_custom_call" | custom-call | tf_op jit(solution)/shard_map/pallas_call | solution.py:341
  98.2 0.6 copy.8
Async XLA Ops:
  0.0 1.0 %copy-start = (bf16[2048,128]{1,0:T(8,128)(2,1)S(1)}, bf16[2048,128]{1,0:T(8,128)(2,1)}, u32[]{:S(2)}) copy-start(bf16[2048,128]{1,0:T(8,128)(2,1)} %s_inv.1) | copy-start | bytes 1572868
  1.0 1.0 %copy-start.1 = (bf16[2048,128]{1,0:T(8,128)(2,1)S(1)}, bf16[2048,128]{1,0:T(8,128)(2,1)}, u32[]{:S(2)}) copy-start(bf16[2048,128]{1,0:T(8,128)(2,1)} %a_inv.1) | copy-start | bytes 1572868
  2.1 0.9 copy-start.2
  3.0 0.9 copy-start.3

commit v2 on v0

v2 whole, which is shorter than its diff:
```python
import jax
import jax.numpy as jnp
from jax import lax
from jax.experimental import pallas as pl
from jax.experimental.pallas import tpu as pltpu
from jax.sharding import PartitionSpec as P

RANK = 16
MESH = pl.DeviceIdType.MESH
BF16, F32 = jnp.bfloat16, jnp.float32
ROWS = 1280
HALF = ROWS // 2
TILE = 320


def place(x, y, z, k):
    return (z * 2 + lax.div(y, 2), x, lax.rem(y, 2) * 2 + k)


def kernel(
    grads, acts, s_inv, a_inv, q_out, q_in, out,
    xv, mbuf, mt, qv, qrel, qg, part, cbuf, lq, both, own, opp, near, hrecv, frecv, pend,
    l_sem, m_send, m_recv, a_send, a_recv, b_send, b_recv, c_send, c_recv,
    d_send, d_recv, e_send, e_recv, f_send, f_recv, h_send, h_recv, n_send, n_recv,
):
    tok, x, pb = lax.axis_index("tok"), lax.axis_index("feat"), lax.axis_index("pb")
    z, k = lax.div(tok, 2), lax.rem(pb, 2)
    y = lax.rem(tok, 2) * 2 + lax.div(pb, 2)
    home, z2 = lax.div(z, 2), lax.rem(z, 2)
    at_home = home == x

    def xs(d):
        return lax.rem(x + d, 4)

    def ys(d):
        return lax.rem(y + d, 4)

    x_dev = [None] + [place(xs(d), y, z, k) for d in (1, 2, 3)]
    y_dev = [None] + [place(x, ys(d), z, k) for d in (1, 2, 3)]
    twin = place(x, y, z, 1 - k)

    def local(src, dst, sem):
        return pltpu.make_async_copy(src, dst, sem)

    def remote(src, dst, send, recv, dev):
        return pltpu.make_async_remote_copy(
            src_ref=src, dst_ref=dst, send_sem=send, recv_sem=recv,
            device_id=dev, device_id_type=MESH,
        )

    sent = []

    def arrived(ref, sem):
        local(ref, ref, sem).wait()

    q_rows = pl.ds(pl.multiple_of(x * 32, 32), 32)
    load_q = [local(q.at[q_rows, :], qv.at[m], l_sem.at[m]) for m, q in enumerate((q_out, q_in))]
    for c in load_q:
        c.start()

    @pl.when(k == 0)
    def _():
        local(s_inv, mbuf.at[0], l_sem.at[2]).start()

    @pl.when(k == 1)
    def _():
        local(a_inv, mbuf.at[1], l_sem.at[2]).start()

    load_x = [local(t, xv.at[m], l_sem.at[3 + m]) for m, t in enumerate((grads, acts))]
    for c in load_x:
        c.start()

    barrier = pltpu.get_barrier_semaphore()

    def greet(dev):
        pl.semaphore_signal(barrier, inc=1, device_id=dev, device_id_type=MESH)

    def greet_source(i, carry):
        sx, sz, sk = lax.div(i, 4), 2 * x + lax.rem(lax.div(i, 2), 2), lax.rem(i, 2)
        me = (sx == x) & (sz == z) & (sk == k)

        @pl.when(jnp.logical_not(me))
        def _():
            greet(place(sx, y, sz, sk))

        return carry

    lax.fori_loop(0, 16, greet_source, 0)
    for dev in (y_dev[1], y_dev[3], x_dev[1], x_dev[2], x_dev[3], twin):
        greet(dev)

    lane = lax.broadcasted_iota(jnp.int32, (8, 128), 1)
    low = lax.broadcasted_iota(jnp.int32, (1, 128), 1) < 64

    def join(a, b):
        return jnp.where(low, a, b)

    def flip(a):
        return pltpu.roll(a, 64, 1)

    for c in load_q:
        c.wait()
    for m in range(2):
        for plane in range(4):
            col = [(plane + d) % 4 * 128 for d in range(4)]
            up, down = (qv[m, :, col[d]:col[d] + 128].astype(F32) for d in (1, 3))
            qrel[m, plane, 0] = qv[m, :, col[2]:col[2] + 128]
            qrel[m, plane, 1] = join(up, flip(down)).astype(BF16)
            qrel[m, plane, 2] = join(flip(up), down).astype(BF16)
            qrel[m, plane, 3] = qv[m, :, col[0]:col[0] + 128]

    arrived(mbuf.at[k], l_sem.at[2])
    mt[pl.ds(pl.multiple_of(k * 128, 128), 128), :] = mbuf[k].T
    pl.semaphore_wait(barrier, 22 - at_home.astype(jnp.int32))

    @pl.when(k == 0)
    def _():
        remote(a_inv, mbuf.at[0], m_send, m_recv, twin).start()

    @pl.when(k == 1)
    def _():
        remote(s_inv, mbuf.at[1], m_send, m_recv, twin).start()

    q_dst_rows = pl.ds(pl.multiple_of(k * 128 + x * 32, 32), 32)
    mine64 = pl.ds(pl.multiple_of(x * 64, 64), 64)
    mb = both.at[k]

    def ship(src, dst, send, recv, dev):
        c = remote(src, dst, send, recv, dev)
        c.start()
        sent.append(c)

    def a_copy(p, i):
        zt, kt = lax.rem(z + 4 + lax.div(i, 2), 8), lax.rem(i, 2)
        me = at_home & (zt == z) & (kt == k)
        src = qrel.at[kt, lax.div(zt, 2), p]
        dst = qg.at[p, z2, y, q_dst_rows, :]
        far = remote(src, dst, a_send.at[p, i], a_recv.at[p], place(home, y, zt, kt))
        return me, local(src, dst, a_recv.at[p]), far

    def d_copy(p, i):
        zt = lax.rem(z + 4 + i, 8)
        me = at_home & (zt == z)
        dst = mb.at[p, z2, y, mine64, :]
        far = remote(lq.at[p], dst, d_send.at[p, i], d_recv.at[p], place(home, y, zt, k))
        return me, local(lq.at[p], dst, d_recv.at[p]), far

    def fan_start(copy, count, p):
        def step(i, carry):
            me, near_copy, far = copy(p, i)

            @pl.when(me)
            def _():
                near_copy.start()

            @pl.when(jnp.logical_not(me))
            def _():
                far.start()

            return carry

        lax.fori_loop(0, count, step, 0)

    def fan_sent(copy, count, p):
        def step(i, carry):
            me, _, far = copy(p, i)

            @pl.when(jnp.logical_not(me))
            def _():
                far.wait_send()

            return carry

        lax.fori_loop(0, count, step, 0)

    def spread(buf, p, send, recv):
        for half, side, d in ((0, 0, 1), (1, 1, 3), (1, 0, 1), (0, 1, 3)):
            mine = buf.at[p, half, y]
            ship(mine, mine, send.at[p, side, half], recv.at[p, side, half], y_dev[d])

    def near_half(buf, p, recv, side, half):
        b = ys(3) if side == 0 else ys(1)
        arrived(buf.at[p, half, b], recv.at[p, side, half])

    def pass_on(buf, p, send, recv):
        for side, d in ((0, 1), (1, 3)):
            near_half(buf, p, recv, side, side)
            half = buf.at[p, side, ys(3) if side == 0 else ys(1)]
            ship(half, half, send.at[p, 2, side], recv.at[p, 2, side], y_dev[d])

    def far_half(buf, p, recv, side):
        arrived(buf.at[p, side, ys(2)], recv.at[p, 2, side])

    def to_twin(p, b, half):
        block = mb.at[p, half, ys(b)]
        ship(block, block, f_send.at[p, b, half], f_recv.at[p, b, half], twin)

    def A(p):
        fan_start(a_copy, 16, p)

    def A_sent(p):
        fan_sent(a_copy, 16, p)

    def B(p):
        arrived(qg.at[p, :, y], a_recv.at[p])
        spread(qg, p, b_send, b_recv)

    def B2(p):
        pass_on(qg, p, b_send, b_recv)

    def C(p):
        for side in range(2):
            near_half(qg, p, b_recv, side, 1 - side)
            far_half(qg, p, b_recv, side)
        part[p] = jnp.dot(mt[...], qg[p].reshape(2048, 128), preferred_element_type=F32)
        for d in (1, 2, 3):
            rows = pl.ds(pl.multiple_of(xs(d) * 64, 64), 64)
            ship(part.at[p, rows, :], cbuf.at[p, d - 1], c_send.at[p, d - 1],
                 c_recv.at[p, d - 1], x_dev[d])

    def D(p):
        for d in range(3):
            arrived(cbuf.at[p, d], c_recv.at[p, d])
        total = part[p, mine64, :] + cbuf[p, 0] + cbuf[p, 1] + cbuf[p, 2]
        lq[p] = total.astype(BF16)
        fan_start(d_copy, 8, p)

    def E(p):
        arrived(mb.at[p, :, y], d_recv.at[p])
        spread(mb, p, e_send, e_recv)
        to_twin(p, 0, 0)
        to_twin(p, 0, 1)

    def E2(p):
        pass_on(mb, p, e_send, e_recv)
        to_twin(p, 3, 0)
        to_twin(p, 1, 1)

    def E3(p):
        for side in range(2):
            near_half(mb, p, e_recv, side, 1 - side)
            to_twin(p, 3 if side == 0 else 1, 1 - side)
        for side in range(2):
            far_half(mb, p, e_recv, side)
            to_twin(p, 2, side)

    def factor():
        c = 1 - k
        arrived(mbuf.at[c], m_recv)
        mt[pl.ds(pl.multiple_of(c * 128, 128), 128), :] = mbuf[c].T

    def acts_in():
        for c in load_x:
            c.wait()

    def twin_in(p):
        for b in range(4):
            for half in range(2):
                arrived(both.at[1 - k, p, half, ys(b)], f_recv.at[p, b, half])

    def tiles(half, body):
        def step(i, carry):
            rows = pl.ds(pl.multiple_of((i + half * (HALF // TILE)) * TILE, TILE), TILE)
            body(rows, pl.ds(pl.multiple_of(i * TILE, TILE), TILE))
            return carry

        lax.fori_loop(0, HALF // TILE, step, 0)

    def project(p, m, rows):
        w = both[m, p].reshape(2048, 128)
        return jnp.dot(xv[m, rows, :], w, preferred_element_type=F32)

    def sides(turn):
        return k if turn == 0 else 1 - k

    def H0(turn):
        m = sides(turn)
        for half in range(2):
            def body(rows, inner):
                opp[m, rows, :] = project(0, m, rows).astype(BF16)

            tiles(half, body)
            side, d = ((1, 3), (0, 1))[half]
            ship(opp.at[m, pl.ds(HALF * half, HALF), :], hrecv.at[side, m],
                 h_send.at[turn, side], h_recv.at[m, side], x_dev[d])

    def to_neighbour(s, half, j):
        rows = pl.ds(HALF * half, HALF)
        ship(near.at[j, s, rows, :], frecv.at[j, s, rows, :], n_send.at[s, half, j],
             n_recv.at[s, half, j], x_dev[1 if j == 0 else 3])

    def H1(s, half):
        def body(rows, inner):
            g, a = (project(s + 1, m, rows) for m in range(2))
            both_ways = join(g, flip(a)), join(flip(g), a)
            near[half, s, rows, :] = both_ways[half].astype(BF16)
            pend[s, half, inner, :] = both_ways[1 - half]

        tiles(half, body)
        to_neighbour(s, half, half)

    def H2(s, half):
        j = 1 - half
        if s == 0:
            for m in range(2):
                arrived(hrecv.at[j, m], h_recv.at[m, j])

        def body(rows, inner):
            g, a = (hrecv[j, m, inner, :].astype(F32) for m in range(2))
            more = join(g, flip(a)) if s == 0 else join(flip(g), a)
            near[j, s, rows, :] = (pend[s, half, inner, :] + more).astype(BF16)

        tiles(half, body)
        to_neighbour(s, half, j)

    def H3(turn):
        m = sides(turn)
        for half in range(2):
            def body(rows, inner):
                own[m, rows, :] = project(3, m, rows)

            tiles(half, body)

    query = lax.broadcasted_iota(jnp.int32, (8, 128), 0)
    pick = jnp.where(lax.div(lane, RANK) == query, 1.0, 0.0).astype(F32)

    def scores(half):
        rows = pl.ds(HALF * half, HALF)
        for s in range(2):
            for j in range(2):
                arrived(frecv.at[j, s, rows, :], n_recv.at[s, half, j])
        first, last = (frecv[0, s, rows, :].astype(F32) + frecv[1, s, rows, :].astype(F32)
                       for s in range(2))
        g = own[0, rows, :] + join(first, flip(last))
        a = own[1, rows, :] + join(flip(first), last)
        prod = g * a * (1.0 / RANK**0.5)
        out[:, rows] = lax.dot_general(
            pick, prod, (((1,), (1,)), ((), ())),
            precision=lax.Precision.HIGHEST, preferred_element_type=F32,
        )

    A(0)
    A(1)
    factor()
    B(0)
    A(2)
    B(1)
    A(3)
    B2(0)
    B(2)
    C(0)
    B2(1)
    B(3)
    D(0)
    C(1)
    B2(2)
    D(1)
    E(0)
    C(2)
    B2(3)
    E2(0)
    D(2)
    E(1)
    C(3)
    E3(0)
    acts_in()
    H0(0)
    E2(1)
    twin_in(0)
    H0(1)
    E(2)
    D(3)
    E3(1)
    twin_in(1)
    H1(0,0)
    E2(2)
    H1(0,1)
    E(3)
    H2(0,0)
    H2(0,1)
    E3(2)
    twin_in(2)
    H1(1,0)
    H1(1,1)
    E2(3)
    H2(1,0)
    H2(1,1)
    E3(3)
    H3(0)
    twin_in(3)
    H3(1)
    scores(0)
    scores(1)

    for c in sent:
        c.wait_send()
    remote(mbuf.at[k], mbuf.at[k], m_send, m_recv, twin).wait_send()
    for p in range(4):
        fan_sent(a_copy, 16, p)
        fan_sent(d_copy, 8, p)


def per_device(out_grads, acts, s_inverse, a_inverse, query_out, query_in):
    dma = pltpu.SemaphoreType.DMA
    vmem = pltpu.VMEM
    return pl.pallas_call(
        kernel,
        out_shape=jax.ShapeDtypeStruct((8, ROWS), F32),
        in_specs=[pl.BlockSpec(memory_space=pl.ANY)] * 6,
        out_specs=pl.BlockSpec(memory_space=pltpu.VMEM),
        scratch_shapes=[
            vmem((2, ROWS, 2048), BF16),
            vmem((2, 2048, 128), BF16),
            vmem((256, 2048), BF16),
            vmem((2, 32, 512), BF16),
            vmem((2, 4, 4, 32, 128), BF16),
            vmem((4, 2, 4, 256, 128), BF16),
            vmem((4, 256, 128), F32),
            vmem((4, 3, 64, 128), F32),
            vmem((4, 64, 128), BF16),
            vmem((2, 4, 2, 4, 256, 128), BF16),
            vmem((2, ROWS, 128), F32),
            vmem((2, ROWS, 128), BF16),
            vmem((2, 2, ROWS, 128), BF16),
            vmem((2, 2, HALF, 128), BF16),
            vmem((2, 2, ROWS, 128), BF16),
            vmem((2, 2, HALF, 128), F32),
            dma((5,)), dma, dma, dma((4, 16)), dma((4,)), dma((4, 3, 2)), dma((4, 3, 2)),
            dma((4, 3)), dma((4, 3)), dma((4, 8)), dma((4,)), dma((4, 3, 2)), dma((4, 3, 2)),
            dma((4, 4, 2)), dma((4, 4, 2)), dma((2, 2)), dma((2, 2)), dma((2, 2, 2)), dma((2, 2, 2)),
        ],
        compiler_params=pltpu.CompilerParams(
            collective_id=0, has_side_effects=True, vmem_limit_bytes=62 * 1024 * 1024
        ),
    )(out_grads, acts, s_inverse, a_inverse, query_out, query_in)


def solution(mesh):
    placed = (
        P(("tok", "pb"), "feat"),
        P(("tok", "pb"), "feat"),
        P("feat", ("tok", "pb")),
        P("feat", ("tok", "pb")),
        P(("tok", "pb"), None),
        P(("tok", "pb"), None),
    )
    return jax.shard_map(
        per_device, mesh=mesh, in_specs=placed, out_specs=P("feat", ("tok", "pb")), check_vma=False
    )
```

time: 285 us -> 81.6 us (0.29)
  waiting for transfers between devices: 203 us -> 0 us
  Pallas kernels: 0 us -> 78.6 us
  blocking collectives: 32.6 us -> 0 us
  matrix products: 21.5 us -> 0 us
  between operations: 13.1 us -> 0.01 us
  other arithmetic: 7.33 us -> 0 us
  starting transfers between devices: 5.56 us -> 0 us
    all_gather x2 -> x0, waiting for transfers between devices: 149 us -> none  [side_by_side(): result, at, outs = (lax.all_gather(both, axis, axis=dim, tiled=True), 0, [])]
    pallas_call x0 -> x1, Pallas kernels: none -> 78.6 us  [per_device(): pl.pallas_call(kernel, out_shape=jax.ShapeDtypeStruct((8, ROWS), F32), in...]
    reduce_scatter x1 -> x0, waiting for transfers between devices: 53.7 us -> none  [in_one_piece(): lax.psum_scatter(both, axis, scatter_dimension=dim, tiled=True)]
    all_to_all x1 -> x0, blocking collectives: 32.6 us -> none  [per_device(): lax.all_to_all(a_inverse, ('tok', 'pb'), split_axis=0, concat_axis=1, til...]
    dot_general x4 -> x0, matrix products: 21.5 us -> none  [the longest x1 6.18 us: per_device(): act_part = jnp.dot(acts, right_block, preferred_element_type=jnp.float32)]
    all_to_all x1 -> x0, starting transfers between devices: 5.48 us -> none  [per_device(): lax.all_to_all(s_inverse, ('tok', 'pb'), split_axis=0, concat_axis=1, til...]
    concatenate x3 -> x0, other arithmetic: 5.29 us -> none  [the longest x1 2.94 us: in_one_piece(): both = jnp.concatenate(arrays, axis=along)]
  transfers between devices with their start and end apart: 4 -> 0, of which waited for: 3 -> 0; matrix products, arithmetic and copies ran while one was open for 2% -> 0% of each run, Pallas kernels for 0% -> 0%
where the time goes in v2:
time: 81.6 us; the launch traced here: 80 us
  Pallas kernels  78.6 us (96%)
  local copies, waits for them, and re-layouts  1.4 us (2%)
    pallas_call x1, Pallas kernels, per_device(): pl.pallas_call(kernel, out_shape=jax.ShapeDtypeStruct((8, ROWS), F32), in...  78.6 us

profile of v2, /device:TPU:3, one launch (start us, length us, event | category | flops | bytes accessed | tf_op | source)
XLA Modules:
  0.0 80.0 jit_solution(9374373707555156274)
XLA Ops:
  0.0 78.6 %shard_map.64 = f32[8,1280]{1,0:T(8,128)} custom-call(bf16[1280,2048]{1,0:T(8,128)(2,1)} %grads.1, bf16[1280,2048]{1,0:T(8,128)(2,1)} %acts.1, bf16[2048,128]{1,0:T(8,128)(2,1)} %s_inv.1, bf16[2048,128]{1,0:T(8,128)(2,1)} %a_inv.1, bf16[128,512]{1,0:T(8,128)(2,1)} %q_out.1, bf16[128,512]{1,0:T(8,128)(2,1)} %q_in.1), custom_call_target="tpu_custom_call" | custom-call | tf_op jit(solution)/shard_map/pallas_call | solution.py:406
  78.6 1.4 %copy.8 = f32[8,1280]{1,0:T(8,128)} copy(f32[8,1280]{1,0:T(8,128)} %shard_map.64) | data formatting | bytes 81920

commit v3 on v2

--- a/solution.py
+++ b/solution.py
@@ -10,7 +10,7 @@
 BF16, F32 = jnp.bfloat16, jnp.float32
 ROWS = 1280
 HALF = ROWS // 2
-TILE = 320
+TILE = 640
 
 
 def place(x, y, z, k):
@@ -48,7 +48,7 @@
             device_id=dev, device_id_type=MESH,
         )
 
-    sent = []
+    sent, last = [], []
 
     def arrived(ref, sem):
         local(ref, ref, sem).wait()
@@ -125,10 +125,10 @@
     mine64 = pl.ds(pl.multiple_of(x * 64, 64), 64)
     mb = both.at[k]
 
-    def ship(src, dst, send, recv, dev):
+    def ship(src, dst, send, recv, dev, to=sent):
         c = remote(src, dst, send, recv, dev)
         c.start()
-        sent.append(c)
+        to.append(c)
 
     def a_copy(p, i):
         zt, kt = lax.rem(z + 4 + lax.div(i, 2), 8), lax.rem(i, 2)
@@ -287,7 +287,7 @@
     def to_neighbour(s, half, j):
         rows = pl.ds(HALF * half, HALF)
         ship(near.at[j, s, rows, :], frecv.at[j, s, rows, :], n_send.at[s, half, j],
-             n_recv.at[s, half, j], x_dev[1 if j == 0 else 3])
+             n_recv.at[s, half, j], x_dev[1 if j == 0 else 3], last)
 
     def H1(s, half):
         def body(rows, inner):
@@ -333,77 +333,83 @@
                        for s in range(2))
         g = own[0, rows, :] + join(first, flip(last))
         a = own[1, rows, :] + join(flip(first), last)
-        prod = g * a * (1.0 / RANK**0.5)
+        prod = g * a
         out[:, rows] = lax.dot_general(
             pick, prod, (((1,), (1,)), ((), ())),
             precision=lax.Precision.HIGHEST, preferred_element_type=F32,
         )
 
     A(0)
+    factor()
+    fan_sent(a_copy, 16, 0)
     A(1)
-    factor()
+    fan_sent(a_copy, 16, 1)
+    A(2)
     B(0)
-    A(2)
+    B2(0)
     B(1)
+    fan_sent(a_copy, 16, 2)
     A(3)
-    B2(0)
-    B(2)
     C(0)
     B2(1)
-    B(3)
+    B(2)
     D(0)
     C(1)
     B2(2)
+    B(3)
     D(1)
-    E(0)
     C(2)
     B2(3)
+    E(0)
+    D(2)
+    C(3)
     E2(0)
-    D(2)
     E(1)
-    C(3)
+    D(3)
     E3(0)
+    E2(1)
+    E(2)
     acts_in()
     H0(0)
-    E2(1)
     twin_in(0)
     H0(1)
-    E(2)
-    D(3)
     E3(1)
+    E(3)
+    E2(2)
     twin_in(1)
     H1(0,0)
-    E2(2)
     H1(0,1)
-    E(3)
+    E3(2)
+    E2(3)
     H2(0,0)
     H2(0,1)
-    E3(2)
     twin_in(2)
     H1(1,0)
     H1(1,1)
-    E2(3)
     H2(1,0)
     H2(1,1)
     E3(3)
     H3(0)
     twin_in(3)
     H3(1)
-    scores(0)
-    scores(1)
-
     for c in sent:
         c.wait_send()
     remote(mbuf.at[k], mbuf.at[k], m_send, m_recv, twin).wait_send()
+    fan_sent(a_copy, 16, 3)
     for p in range(4):
-        fan_sent(a_copy, 16, p)
         fan_sent(d_copy, 8, p)
+
+    scores(0)
+    scores(1)
+
+    for c in last:
+        c.wait_send()
 
 
 def per_device(out_grads, acts, s_inverse, a_inverse, query_out, query_in):
     dma = pltpu.SemaphoreType.DMA
     vmem = pltpu.VMEM
-    return pl.pallas_call(
+    summed = pl.pallas_call(
         kernel,
         out_shape=jax.ShapeDtypeStruct((8, ROWS), F32),
         in_specs=[pl.BlockSpec(memory_space=pl.ANY)] * 6,
@@ -433,6 +439,7 @@
             collective_id=0, has_side_effects=True, vmem_limit_bytes=62 * 1024 * 1024
         ),
     )(out_grads, acts, s_inverse, a_inverse, query_out, query_in)
+    return summed * (1.0 / RANK**0.5)
 
 
 def solution(mesh):

time: 81.6 us -> 80.5 us (0.987); the launches traced: 80 us -> 80.4 us
  other arithmetic: 0 us -> 1.4 us
  local copies, waits for them, and re-layouts: 1.4 us -> 0 us
    mul x0 -> x1, other arithmetic: none -> 1.4 us  [per_device(): return summed * (1.0 / RANK ** 0.5)]
    unnamed x1 -> x0, local copies, waits for them, and re-layouts: 1.4 us -> none
where the time goes in v3:
time: 80.5 us; the launch traced here: 80.4 us
  Pallas kernels  78.9 us (98%)
  other arithmetic  1.4 us (2%)
    pallas_call x1, Pallas kernels, per_device(): pl.pallas_call(kernel, out_shape=jax.ShapeDtypeStruct((8, ROWS), F32), in...  78.9 us

profile of v3, /device:TPU:3, one launch (start us, length us, event | category | flops | bytes accessed | tf_op | source)
XLA Modules:
  0.0 80.4 jit_solution(14304264702549425443)
XLA Ops:
  0.0 78.9 %shard_map.64 = f32[8,1280]{1,0:T(8,128)} custom-call(bf16[1280,2048]{1,0:T(8,128)(2,1)} %grads.1, bf16[1280,2048]{1,0:T(8,128)(2,1)} %acts.1, bf16[2048,128]{1,0:T(8,128)(2,1)} %s_inv.1, bf16[2048,128]{1,0:T(8,128)(2,1)} %a_inv.1, bf16[128,512]{1,0:T(8,128)(2,1)} %q_out.1, bf16[128,512]{1,0:T(8,128)(2,1)} %q_in.1), custom_call_target="tpu_custom_call" | custom-call | tf_op jit(solution)/shard_map/pallas_call | solution.py:412
  79.0 1.4 %broadcast_multiply_fusion = f32[8,1280]{1,0:T(8,128)} fusion(f32[8,1280]{1,0:T(8,128)} %shard_map.64), kind=kLoop, calls=%fused_computation | loop fusion | flops 10240 | bytes 81920 | tf_op jit(solution)/shard_map/mul | solution.py:442

commit v4 on v3

--- a/solution.py
+++ b/solution.py
@@ -275,11 +275,8 @@
 
     def H0(turn):
         m = sides(turn)
+        opp[m] = project(0, m, pl.ds(0, ROWS)).astype(BF16)
         for half in range(2):
-            def body(rows, inner):
-                opp[m, rows, :] = project(0, m, rows).astype(BF16)
-
-            tiles(half, body)
             side, d = ((1, 3), (0, 1))[half]
             ship(opp.at[m, pl.ds(HALF * half, HALF), :], hrecv.at[side, m],
                  h_send.at[turn, side], h_recv.at[m, side], x_dev[d])

time: 80.5 us -> 80.2 us (level)
  no operation moved by 1% of the time
where the time goes in v4:
time: 80.2 us; the launch traced here: 80.1 us
  Pallas kernels  78.7 us (98%)
  other arithmetic  1.4 us (2%)
    pallas_call x1, Pallas kernels, per_device(): pl.pallas_call(kernel, out_shape=jax.ShapeDtypeStruct((8, ROWS), F32), in...  78.7 us

profile of v4, /device:TPU:3, one launch (start us, length us, event | category | flops | bytes accessed | tf_op | source)
XLA Modules:
  0.0 80.1 jit_solution(9666722565353423882)
XLA Ops:
  0.0 78.7 %shard_map.64 = f32[8,1280]{1,0:T(8,128)} custom-call(bf16[1280,2048]{1,0:T(8,128)(2,1)} %grads.1, bf16[1280,2048]{1,0:T(8,128)(2,1)} %acts.1, bf16[2048,128]{1,0:T(8,128)(2,1)} %s_inv.1, bf16[2048,128]{1,0:T(8,128)(2,1)} %a_inv.1, bf16[128,512]{1,0:T(8,128)(2,1)} %q_out.1, bf16[128,512]{1,0:T(8,128)(2,1)} %q_in.1), custom_call_target="tpu_custom_call" | custom-call | tf_op jit(solution)/shard_map/pallas_call | solution.py:409
  78.7 1.4 %broadcast_multiply_fusion = f32[8,1280]{1,0:T(8,128)} fusion(f32[8,1280]{1,0:T(8,128)} %shard_map.64), kind=kLoop, calls=%fused_computation | loop fusion | flops 10240 | bytes 81920 | tf_op jit(solution)/shard_map/mul | solution.py:439
